TPU v7x, 32 devices: a whole 2x2x4 slice. The times are simulated.
32 devices in a mesh: patch: 16 (over z, y, x), frame: 2 (over core).
Axes of the slice: x: 2, y: 2, z: 4, core: 2. Of those that a mesh axis runs over, the one named last changes fastest.
Arguments:
- basis: bfloat16 [3, 4096, 1024], P(None, 'patch'), may hold values from -0.25 to 0.25
- latents: bfloat16 [1024, 1024], P('frame', 'patch'), may hold values from -2 to 2
- rest_pos: float32 [3, 4096], P(None, 'patch'), may hold values from -3 to 3
- triangles: int32 [3, 8192], P(None, 'patch'), may hold values from 0 to 511
- hinges: int32 [4, 6144], P(None, 'patch'), may hold values from 0 to 511
- rest_sq: float32 [3, 8192], P(None, 'patch'), may hold values from 0.5 to 3
- bend_rest: float32 [3, 6144], P(None, 'patch'), may hold values from -5 to 5
- masses: float32 [4096], P('patch'), may hold values from 0.5 to 2
- send_rows: int32 [2, 2048], P(None, 'patch'), may hold values from 0 to 255, as said below
Outputs:
- basis_grad: float32 [3, 4096, 1024], P(None, ('patch', 'frame'))
- latent_grad: float32 [1024, 1024], P('frame', 'patch')
Inputs may be any that keep to these rules, and one draw needn't show every extreme that they name: `send_rows`: within one patch's columns the 256 entries of both rows are distinct own vertex numbers.
All inputs are finite; a program needn't handle non-finite values.
Results may differ from a plain program's by a relative error of at most 0.006.
Values may be sent and summed in bfloat16 or wider, within the bound.
A program may use at most 64 MiB of HBM per device.

v0:
```python
import functools

import jax
import jax.numpy as jnp
from jax import lax
from jax.experimental import pallas as pl
from jax.experimental.pallas import tpu as pltpu
from jax.sharding import PartitionSpec as P

MEMBRANE = 5.0
BENDING = 5.0
GRAVITY = 40.0
BF = jnp.bfloat16
F32 = jnp.float32


def hot(rows, ids):
    iota = lax.broadcasted_iota(jnp.int32, (rows, ids.shape[0]), 0)
    return (iota == ids[None, :]).astype(F32)


def mm(a, b, dims):
    return lax.dot_general(a, b, (dims, ((), ())), preferred_element_type=F32)


def exact(a, b):
    return jnp.dot(a, b, precision=lax.Precision.HIGHEST, preferred_element_type=F32)


PLANE = 4
MESH_ID = pl.DeviceIdType.MESH
DMA = pltpu.SemaphoreType.DMA


def places(n):
    p = lax.axis_index("patch")
    xnb = p + 1 - 2 * (p % 2)
    ynb = p + 2 - 4 * ((p // 2) % 2)
    return p, p // PLANE, p % PLANE, xnb, ynb


def greet(peers, pos=None):
    bar = pltpu.get_barrier_semaphore()
    if pos is not None:
        pl.semaphore_signal(bar, inc=1, device_id={"frame": 1 - pos}, device_id_type=MESH_ID)
    for q in peers:
        pl.semaphore_signal(bar, inc=1, device_id={"patch": q}, device_id_type=MESH_ID)
    pl.semaphore_wait(bar, len(peers) + (pos is not None))


def send(src, dst, ss, rs, q):
    return pltpu.make_async_remote_copy(
        src_ref=src, dst_ref=dst, send_sem=ss, recv_sem=rs,
        device_id={"patch": q}, device_id_type=MESH_ID,
    )


def gather_kernel(
    n, w, x_ref, b0, b1, b2, sel_ref, r_ref, o_ref, d_ref, t_ref, hb, he,
    zs, zr, xs, xr, ys, yr, rs, rr, hds, hdr, fs, fr, qs, qr
):
    hi = n // PLANE
    p, h, lo, xnb, ynb = places(n)
    pos = lax.axis_index("frame")
    lox, loy = xnb % PLANE, ynb % PLANE
    ring = [(p + n - 1) % n, (p + 1) % n]
    bs = (b0, b1, b2)
    vs = b0.shape[0]
    ff = x_ref.shape[1]
    hs = sel_ref.shape[1] // 4

    def rows(hh, ll):
        return o_ref.at[pl.ds(pl.multiple_of((hh * PLANE + ll) * w, w), w)]

    def half(ref, c, d, which):
        return ref.at[c, pl.ds(pl.multiple_of((2 * d + which) * hs, hs), hs)]

    zpeer = [((h + j) % hi) * PLANE + lo for j in range(hi)]
    greet(zpeer[1:] + [xnb, ynb] + ring, pos)
    order = sorted(range(1, hi), key=lambda j: min(j, hi - j))
    mine = rows(h, lo)
    zc = {j: send(x_ref, mine, zs.at[j], zr.at[j], zpeer[j]) for j in order}
    xc, yc, rc, hc, fc = {}, {}, {}, {}, {}
    xc[0] = send(x_ref, mine, xs.at[0], xr.at[0], xnb)
    yc[0] = send(x_ref, mine, ys.at[0], yr.at[0], ynb)
    xc[0].start()
    yc[0].start()
    for j in reversed(order):
        zc[j].start()
    rest = [send(r_ref.at[d], t_ref.at[1 - d], qs.at[d], qr.at[d], ring[d]) for d in range(2)]
    rest[0].start()
    rest[1].start()

    def halo(c):
        for d in range(2):
            hc[c, d] = send(
                half(hb, c, d, pos), half(he, c, 1 - d, pos),
                hds.at[2 * c + d], hdr.at[2 * c + d], ring[d],
            )
            hc[c, d].start()

    def swap(c):
        for d in range(2):
            hc[c, d].wait_recv()
            part = half(he, c, 1 - d, pos)
            fc[c, d] = pltpu.make_async_remote_copy(
                src_ref=part, dst_ref=part,
                send_sem=fs.at[2 * c + d], recv_sem=fr.at[2 * c + d],
                device_id={"frame": 1 - pos}, device_id_type=MESH_ID,
            )
            fc[c, d].start()

    def decode(c, src, at, count):
        d_ref[at : at + count, c * ff : (c + 1) * ff] = mm(
            src, o_ref[...], ((1,), (0,))
        ).astype(BF)

    def far(c):
        fc[c, 0].wait_recv()
        fc[c, 1].wait_recv()
        decode(c, he[c], vs, 4 * hs)

    for c in range(3):
        hb[c] = mm(sel_ref[...], bs[c][...], ((0,), (0,))).astype(BF)
        if c == 0:
            halo(0)
    mine[...] = x_ref[...]

    def relay(j):
        hh = (h + hi - j) % hi
        (yc if j % 2 else xc)[j].wait_recv()
        part = rows(hh, loy if j % 2 else lox)
        rc[j] = send(part, part, rs.at[j], rr.at[j], xnb if j % 2 else ynb)
        rc[j].start()

    last = 0
    for at, j in enumerate(order):
        zc[j].wait_recv()
        part = rows((h + hi - j) % hi, lo)
        xc[j] = send(part, part, xs.at[j], xr.at[j], xnb)
        yc[j] = send(part, part, ys.at[j], yr.at[j], ynb)
        xc[j].start()
        yc[j].start()
        if at == 1:
            halo(1)
        relay(last)
        last = j
    if len(order) < 2:
        halo(1)
    relay(last)
    halo(2)
    for j in range(hi):
        (xc if j % 2 else yc)[j].wait_recv()
        rc[j].wait_recv()
    swap(0)
    for c in range(3):
        decode(c, bs[c][...], 0, vs)
    swap(1)
    far(0)
    swap(2)
    far(1)
    far(2)
    for d in range(2):
        rest[d].wait_recv()
        rest[d].wait_send()
    for c in range(3):
        for d in range(2):
            fc[c, d].wait_send()
            hc[c, d].wait_send()
    for j in range(hi):
        if j:
            zc[j].wait_send()
        xc[j].wait_send()
        yc[j].wait_send()
        rc[j].wait_send()


def gather_all(x, bases, sel, rsend, n):
    w, f = x.shape
    hi = n // PLANE
    vs, kk = bases[0].shape
    slots = sel.shape[1]
    vm = pl.BlockSpec(memory_space=pltpu.VMEM)
    return pl.pallas_call(
        functools.partial(gather_kernel, n, w),
        out_shape=[
            jax.ShapeDtypeStruct((n * w, f), x.dtype),
            jax.ShapeDtypeStruct((vs + slots, 3 * f), x.dtype),
            jax.ShapeDtypeStruct(rsend.shape, rsend.dtype),
        ],
        in_specs=[vm] * 6,
        out_specs=[vm] * 3,
        scratch_shapes=[pltpu.VMEM((3, slots, kk), x.dtype)] * 2
        + [DMA((hi,))] * 8 + [DMA((6,))] * 4 + [DMA((2,))] * 2,
        compiler_params=pltpu.CompilerParams(
            collective_id=0, has_side_effects=True, vmem_limit_bytes=60000 * 1024
        ),
    )(x, *bases, sel, rsend)


def tail_kernel(
    n, w, own_ref, gh_ref, sel_ref, b0, b1, b2, lt_ref, lo_ref, bg_ref, o_ref,
    bt, bk, adj, got, acc, g, rl, sb, cx, cy, zb, zl,
    ks, kr, ps, pr, ls, lr, xs, xr, ys, yr, zs, zr,
):
    hi = n // PLANE
    p, h, lo, xnb, ynb = places(n)
    pos = lax.axis_index("frame")
    lox, loy = xnb % PLANE, ynb % PLANE
    lod = PLANE - 1 - lo
    ring = [(p + n - 1) % n, (p + 1) % n]
    bs = (b0, b1, b2)
    vs, kk = b0.shape
    ff = lt_ref.shape[1]
    halo = gh_ref.shape[0] // 2
    half = vs // 2
    tile = 256

    def rows(j, ll):
        hh = (h + j) % hi
        return g.at[pl.ds(pl.multiple_of((hh * PLANE + ll) * w, w), w)]

    zpeer = [((h + j) % hi) * PLANE + lo for j in range(hi)]
    greet(zpeer[1:] + [xnb, ynb] + ring, pos)
    kc, pc = {}, []
    for c in range(3):
        for d in range(2):
            kc[c, d] = send(
                gh_ref.at[pl.ds(d * halo, halo), pl.ds(c * ff, ff)],
                bk.at[c, pl.ds((1 - d) * halo, halo)],
                ks.at[2 * c + d], kr.at[2 * c + d], ring[d],
            )
            kc[c, d].start()
    for c in range(3):
        bt[c] = bs[c][...].T
    for c in range(3):
        kc[c, 0].wait_recv()
        kc[c, 1].wait_recv()
        adj[c] = (
            own_ref[:, pl.ds(c * ff, ff)] + mm(sel_ref[...], bk[c], ((1,), (0,)))
        ).astype(BF)
        cp = pltpu.make_async_remote_copy(
            src_ref=adj.at[c, pl.ds(pl.multiple_of((1 - pos) * half, half), half)],
            dst_ref=got.at[c], send_sem=ps.at[c], recv_sem=pr.at[c],
            device_id={"frame": 1 - pos}, device_id_type=MESH_ID,
        )
        cp.start()
        pc.append(cp)
        for r in range(0, kk, tile):
            block = mm(bt[c, r : r + tile], adj[c], ((1,), (0,)))
            if c:
                block = block + acc[r : r + tile]
            if c < 2:
                acc[r : r + tile] = block
            else:
                g[r : r + tile] = block.astype(BF)

    def grad(c):
        mine = adj[c, pl.ds(pl.multiple_of(pos * half, half), half)]
        for r in range(0, kk, tile):
            one = mm(mine, lt_ref[r : r + tile], ((1,), (1,))).astype(BF).astype(F32)
            two = mm(got[c], lo_ref[r : r + tile], ((1,), (1,))).astype(BF).astype(F32)
            bg_ref[c, :, r : r + tile] = one + two

    order = sorted(range(1, hi), key=lambda j: -min(j, hi - j))
    even = [j for j in order if j % 2 == 0]
    odd = [j for j in order if j % 2]
    lc, xc, yc, zc = {}, {}, {}, {}

    def via(j):
        lc[j] = send(rows(j, lod), rl.at[j], ls.at[j], lr.at[j], ynb if j % 2 else xnb)
        lc[j].start()

    def to_x(j, src):
        xc[j] = send(src, cx.at[j], xs.at[j], xr.at[j], xnb)
        xc[j].start()

    def to_y(j, src):
        yc[j] = send(src, cy.at[j], ys.at[j], yr.at[j], ynb)
        yc[j].start()

    def summed(j):
        lc[j].wait_recv()
        own = rows(j, lox if j % 2 else loy)
        sb[j] = (own[...].astype(F32) + rl[j].astype(F32)).astype(BF)
        (to_x if j % 2 else to_y)(j, sb.at[j])

    def total(j):
        xc[j].wait_recv()
        yc[j].wait_recv()
        return rows(j, lo)[...].astype(F32) + cx[j].astype(F32) + cy[j].astype(F32)

    for j in even:
        via(j)
    for j in odd:
        via(j)
    for j in even:
        to_x(j, rows(j, lox))
    for c in range(3):
        pc[c].wait_recv()
    grad(0)
    for j in even:
        summed(j)
    for j in odd:
        to_y(j, rows(j, loy))
    for j in odd:
        summed(j)
    via(0)
    to_x(0, rows(0, lox))
    grad(1)
    for j in order:
        zb[j] = total(j).astype(BF)
        zc[j] = send(zb.at[j], zl.at[j], zs.at[j], zr.at[j], zpeer[j])
        zc[j].start()
    summed(0)
    grad(2)
    s = total(0)
    for j in reversed(order):
        zc[j].wait_recv()
        s = s + zl[j].astype(F32)
    o_ref[...] = s
    for c in range(3):
        kc[c, 0].wait_send()
        kc[c, 1].wait_send()
        pc[c].wait_send()
    for j in [0] + order:
        lc[j].wait_send()
        xc[j].wait_send()
        yc[j].wait_send()
        if j:
            zc[j].wait_send()


def tail(own, gh, sel, bases, lat_t, lat_o, n):
    kk, f = lat_t.shape
    w = kk // n
    hi = n // PLANE
    vs = own.shape[0]
    vm = pl.BlockSpec(memory_space=pltpu.VMEM)
    vmem = pltpu.VMEM
    return pl.pallas_call(
        functools.partial(tail_kernel, n, w),
        out_shape=[
            jax.ShapeDtypeStruct((3, vs // 2, kk), F32),
            jax.ShapeDtypeStruct((w, f), F32),
        ],
        in_specs=[vm] * 8,
        out_specs=[vm] * 2,
        scratch_shapes=[
            vmem((3, kk, vs), BF),
            vmem((3, gh.shape[0], f), BF),
            vmem((3, vs, f), BF),
            vmem((3, vs // 2, f), BF),
            vmem((kk, f), F32),
            vmem((kk, f), BF),
        ]
        + [vmem((hi, w, f), BF)] * 6
        + [DMA((6,))] * 2
        + [DMA((3,))] * 2
        + [DMA((hi,))] * 8,
        compiler_params=pltpu.CompilerParams(
            collective_id=1, has_side_effects=True, vmem_limit_bytes=60000 * 1024
        ),
    )(own, gh, sel, *bases, lat_t, lat_o)


def local(basis, latents, rest_pos, triangles, hinges, rest_sq, bend_rest, masses, send_rows):
    vs = basis.shape[1]
    ff = latents.shape[0]
    halo = send_rows.shape[1]
    nt = triangles.shape[1]
    total = ff * lax.axis_size("frame")
    pos = lax.axis_index("frame")
    n = lax.axis_size("patch")
    ext = vs + 2 * halo
    ta, tb, tc = (hot(ext, triangles[i]) for i in range(3))
    ha, hb, hc, hd = (hot(ext, hinges[i]) for i in range(4))
    inc = jnp.concatenate([tb - ta, tc - tb, hc + hd - ha - hb], axis=1).astype(BF)
    self32 = hot(vs, send_rows.reshape(-1))
    sel = self32.astype(BF)
    rest_out = exact(rest_pos, self32)
    bases = [basis[c] for c in range(3)]
    rsend = jnp.pad(rest_out.reshape(3, 2, halo).transpose(1, 0, 2), ((0, 0), (0, 5), (0, 0)))
    lat_t, dext, rhalo = gather_all(latents.T, bases, sel, rsend, n)
    lat_o = lax.ppermute(lat_t, "frame", [(0, 1), (1, 0)])
    rest_ext = jnp.concatenate([rest_pos, rhalo[0, :3], rhalo[1, :3]], axis=1)
    rest_edge = exact(rest_ext, inc.astype(F32))
    rest_edge = rest_edge.at[:, 2 * nt :].add(-bend_rest)
    edges = mm(inc, dext, ((0,), (0,)))
    e1 = [edges[:nt, c * ff : (c + 1) * ff] + rest_edge[c, :nt, None] for c in range(3)]
    e2 = [edges[nt : 2 * nt, c * ff : (c + 1) * ff] + rest_edge[c, nt : 2 * nt, None] for c in range(3)]
    hh = [edges[2 * nt :, c * ff : (c + 1) * ff] + rest_edge[c, 2 * nt :, None] for c in range(3)]
    e3 = [-(a + b) for a, b in zip(e1, e2)]
    k = 4.0 * MEMBRANE / total

    def strain(e, r):
        return k * (e[0] * e[0] + e[1] * e[1] + e[2] * e[2] - r[:, None])

    s1, s2, s3 = strain(e1, rest_sq[0]), strain(e2, rest_sq[1]), strain(e3, rest_sq[2])
    u1 = jnp.concatenate([s1 * e1[c] - s3 * e3[c] for c in range(3)], axis=1)
    u2 = jnp.concatenate([s2 * e2[c] - s3 * e3[c] for c in range(3)], axis=1)
    uh = jnp.concatenate(hh, axis=1) * (2.0 * BENDING / total)
    forces = jnp.concatenate([u1, u2, uh], axis=0).astype(BF)
    g = mm(inc, forces, ((1,), (0,)))
    gh = g[vs:].astype(BF)
    owned = g[:vs].at[:, 2 * ff :].add((GRAVITY / total) * masses[:, None])
    basis_grad, lg = tail(owned, gh, sel, bases, lat_t, lat_o, n)
    return (basis_grad, lg.T)


def solution(mesh):
    return jax.shard_map(
        local,
        mesh=mesh,
        in_specs=(
            P(None, "patch", None),
            P("frame", "patch"),
            P(None, "patch"),
            P(None, "patch"),
            P(None, "patch"),
            P(None, "patch"),
            P(None, "patch"),
            P("patch"),
            P(None, "patch"),
        ),
        out_specs=(P(None, ("patch", "frame"), None), P("frame", "patch")),
        check_vma=False,
    )
```

profile of v0, /device:TPU:0, one launch (start us, length us, event | category | flops | bytes accessed | tf_op | source)
XLA Modules:
  0.0 101.4 jit_solution(13481424174635363233)
XLA Ops:
  0.6 0.0 copy-start.7
  0.6 0.0 copy-start.10
  0.7 0.0 copy-start.3
  0.7 0.0 copy-start.5
  0.7 2.6 %slice_bitcast_fusion = (bf16[256,1024]{1,0:T(8,128)(2,1)}, bf16[256,1024]{1,0:T(8,128)(2,1)}, bf16[256,1024]{1,0:T(8,128)(2,1)}) fusion(bf16[3,256,1024]{2,1,0:T(8,128)(2,1)} %param.13), kind=kLoop, calls=%fused_computation.57 | loop fusion | bytes 3145728 | tf_op jit(solution)/shard_map/squeeze | solution.py:382
  3.3 0.0 copy-done.7
  3.3 0.7 convert_convert_fusion.sel_ref
  3.9 0.0 copy-done.10
  3.9 0.1 convolution_bitcast_fusion
  4.1 0.7 pad.8.r_ref
  4.7 38.9 %shard_map.104 = (bf16[1024,512]{1,0:T(8,128)(2,1)}, bf16[512,1536]{1,0:T(8,128)(2,1)}, f32[2,8,128]{2,1,0:T(8,128)}) custom-call(bf16[64,512]{1,0:T(8,128)(2,1)} %bitcast.34, bf16[256,1024]{1,0:T(8,128)(2,1)} %get-tuple-element.59.b0, bf16[256,1024]{1,0:T(8,128)(2,1)} %get-tuple-element.60.b1, bf16[256,1024]{1,0:T(8,128)(2,1)} %get-tuple-element.58.b2, ...), custom_call_target="tpu_custom_call" | custom-call | tf_op jit(solution)/shard_map/pallas_call | solution.py:184
  43.7 0.0 copy-start.9
  43.7 0.1 collective-permute-start
  43.8 0.8 slice_bitcast_fusion.4
  44.6 0.0 copy-done.3
  44.6 0.0 copy-done.5
  44.7 0.4 fusion.15
  45.1 0.4 subtract_convert_fusion.6
  45.5 0.7 fusion.22
  46.2 0.0 copy-done.9
  46.2 0.0 copy-start.6
  46.2 0.0 copy-start.4
  46.2 2.5 %fusion.30 = f32[1408,1536]{1,0:T(8,128)S(1)} fusion(bf16[512,1536]{1,0:T(8,128)(2,1)S(1)} %copy-done.9, bf16[512,384]{1,0:T(8,128)(2,1)S(1)} %subtract_convert_fusion.6, bf16[512,512]{1,0:T(8,128)(2,1)S(1)} %get-tuple-element.76, bf16[512,512]{1,0:T(8,128)(2,1)S(1)} %get-tuple-element.75), kind=kOutput, calls=%fused_computation.82 | convolution fusion | flops 2218917888 | bytes 11665408 | tf_op jit(solution)/shard_map/dot_general | solution.py:23
  48.7 0.0 copy-done.6
  48.7 0.0 copy-done.4
  48.8 1.4 %subtract_convert_fusion.5 = (bf16[512,512]{1,0:T(8,128)(2,1)S(1)}, f32[512,512]{1,0:T(8,128)S(1)}, f32[512,512]{1,0:T(8,128)S(1)}, f32[512,512]{1,0:T(8,128)S(1...) fusion(f32[1408,1536]{1,0:T(8,128)S(1)} %fusion.30, f32[512]{0:T(512)S(1)} %bitcast.47, f32[512]{0:T(512)S(1)} %bitcast.49, ...), kind=kLoop, calls=%fused_computation.37 | loop fusion | flops 7340032 | bytes 12075008 | tf_op jit(solution)/shard_map/convert.7
  50.2 0.6 subtract_convert_fusion.2
  50.8 0.2 slice_add_fusion.8
  51.0 0.1 fusion.14
  51.2 0.8 subtract_convert_fusion.4
  52.0 2.6 %fusion = f32[512,1536]{1,0:T(8,128)S(1)} fusion(bf16[384,1536]{1,0:T(8,128)(2,1)S(1)} %fusion.14, bf16[512,512]{1,0:T(8,128)(2,1)S(1)} %get-tuple-element.53, bf16[512,512]{1,0:T(8,128)(2,1)S(1)} %get-tuple-element.52, bf16[512,512]{1,0:T(8,128)(2,1)S(1)} %get-tuple-element.49, bf16[512,512]{1,0:T(8,128)(2,1)S(1)} %get-tuple-element.54, ...), kind=kOutput, calls=%fused_computation | convolution fusion | flops 2249195520 | bytes 8912896 | tf_op jit(solution)/shard_map/dot_general | solution.py:23
  54.7 0.0 copy-start.8
  54.7 0.1 slice.204
  54.8 1.0 slice.269.gh_ref
  55.7 0.0 copy-done.8
  55.7 0.1 fusion.20.own_ref
  55.9 0.0 copy-start
  55.9 0.0 collective-permute-done.lo_ref
  55.9 1.1 %copy-done = f32[256,1536]{1,0:T(8,128)} copy-done((f32[256,1536]{1,0:T(8,128)}, f32[256,1536]{1,0:T(8,128)S(1)}, u32[]{:S(2)}) %copy-start) | copy-done | bytes 1572888
  57.0 0.0 copy-start.1
  57.0 1.0 copy-done.1
  58.0 40.0 %shard_map.105 = (f32[3,128,1024]{2,1,0:T(8,128)}, f32[64,512]{1,0:T(8,128)}) custom-call(f32[256,1536]{1,0:T(8,128)} %copy-done, bf16[256,1536]{1,0:T(8,128)(2,1)} %slice.269.gh_ref, bf16[256,256]{1,0:T(8,128)(2,1)} %convert_convert_fusion.sel_ref, bf16[256,1024]{1,0:T(8,128)(2,1)} %get-tuple-element.59.b0, bf16[256,1024]{1,0:T(8,128)(2,1)} %get-tuple-element.60.b1, ...), custom_call_target="tpu_custom_call" | custom-call | tf_op jit(solution)/shard_map/pallas_call | solution.py:341
  98.0 0.0 copy-start.2
  98.0 2.8 %copy.14 = f32[3,128,1024]{2,1,0:T(8,128)} copy(f32[3,128,1024]{2,1,0:T(8,128)} %get-tuple-element.79) | data formatting | bytes 3145728
  100.7 0.0 copy-done.2
  100.7 0.7 copy.15
  (7 shorter events, 0.1 us)
Async XLA Ops:
  0.6 2.6 %copy-start.7 = (s32[2,128]{1,0:T(2,128)S(1)}, s32[2,128]{1,0:T(2,128)}, u32[]{:S(2)}) copy-start(s32[2,128]{1,0:T(2,128)} %param.21) | copy-start | bytes 3076
  0.6 3.3 %copy-start.10 = (f32[3,256]{1,0:T(4,128)S(1)}, f32[3,256]{1,0:T(4,128)}, u32[]{:S(2)}) copy-start(f32[3,256]{1,0:T(4,128)} %param.15) | copy-start | bytes 9220
  0.7 43.9 %copy-start.3 = (s32[4,384]{1,0:T(4,128)S(1)}, s32[4,384]{1,0:T(4,128)}, u32[]{:S(2)}) copy-start(s32[4,384]{1,0:T(4,128)} %param.17) | copy-start | bytes 18436
  0.7 44.0 %copy-start.5 = (s32[3,512]{1,0:T(4,128)S(1)}, s32[3,512]{1,0:T(4,128)}, u32[]{:S(2)}) copy-start(s32[3,512]{1,0:T(4,128)} %param.16) | copy-start | bytes 18436
  43.7 2.5 %copy-start.9 = (bf16[512,1536]{1,0:T(8,128)(2,1)S(1)}, bf16[512,1536]{1,0:T(8,128)(2,1)}, u32[]{:S(2)}) copy-start(bf16[512,1536]{1,0:T(8,128)(2,1)} %get-tuple-element.31) | copy-start | bytes 4718596
  43.7 12.2 %collective-permute-start = (bf16[1024,512]{1,0:T(8,128)(2,1)}, bf16[1024,512]{1,0:T(8,128)(2,1)S(1)}, u32[]{:S(2)}, u32[]{:S(2)}) collective-permute-start(bf16[1024,512]{1,0:T(8,128)(2,1)} %get-tuple-element.33.lt_ref), channel_id=1, source_target_pairs={{0,1},{1,0},{2,3},{3,2},{4,5},{5,4},{6,7},{7,6},{8,9},{9,8},{10,11... | collective-permute-start | bytes 3145736 | tf_op jit(solution)/shard_map/ppermute | solution.py:385
  46.2 2.5 %copy-start.6 = (f32[3,512]{1,0:T(4,128)S(1)}, f32[3,512]{1,0:T(4,128)}, u32[]{:S(2)}) copy-start(f32[3,512]{1,0:T(4,128)} %param.18) | copy-start | bytes 18436
  46.2 2.5 %copy-start.4 = (f32[3,384]{1,0:T(4,128)S(1)}, f32[3,384]{1,0:T(4,128)}, u32[]{:S(2)}) copy-start(f32[3,384]{1,0:T(4,128)} %param.19) | copy-start | bytes 13828
  54.7 1.1 %copy-start.8 = (f32[256]{0:T(256)S(1)}, f32[256]{0:T(256)}, u32[]{:S(2)}) copy-start(f32[256]{0:T(256)} %param.20) | copy-start | bytes 3076
  55.9 1.1 %copy-start = (f32[256,1536]{1,0:T(8,128)}, f32[256,1536]{1,0:T(8,128)S(1)}, u32[]{:S(2)}) copy-start(f32[256,1536]{1,0:T(8,128)S(1)} %fusion.20.own_ref) | copy-start | bytes 4718596
  57.0 1.0 copy-start.1
  98.0 2.8 %copy-start.2 = (f32[64,512]{1,0:T(8,128)S(1)}, f32[64,512]{1,0:T(8,128)}, u32[]{:S(2)}) copy-start(f32[64,512]{1,0:T(8,128)} %get-tuple-element.35) | copy-start | bytes 393220
where the time goes:
time: 102 us; the launch traced here: 101 us
  Pallas kernels  78.9 us (77%)
  local copies, waits for them, and re-layouts  10.8 us (11%)
  matrix products  5.88 us (6%)
  other arithmetic  4.87 us (5%)
    pallas_call x1, Pallas kernels, tail(): pl.pallas_call(functools.partial(tail_kernel, n, w), out_shape=[jax.Shape...  40 us
    pallas_call x1, Pallas kernels, gather_all(): pl.pallas_call(functools.partial(gather_kernel, n, w), out_shape=[jax.Sha...  38.9 us
    unnamed x24, local copies, waits for them, and re-layouts  5.58 us
    dot_general x2, matrix products, mm(): return lax.dot_general(a, b, (dims, ((), ())), preferred_element_type=F32)  5.07 us
    another operation x6, other arithmetic  3.85 us
    squeeze x1, local copies, waits for them, and re-layouts, local(): bases = [basis[c] for c in range(3)]  2.58 us
  transfers between devices with their start and end apart: 1, of which 0 were waited for; matrix products, arithmetic and copies ran while one was open for 12% of the time, Pallas kernels for 0%

commit v1 on v0

--- a/solution.py
+++ b/solution.py
@@ -56,7 +56,7 @@
 
 
 def gather_kernel(
-    n, w, x_ref, b0, b1, b2, sel_ref, r_ref, o_ref, d_ref, t_ref, hb, he,
+    n, w, x_ref, b_ref, sel_ref, r_ref, o_ref, d_ref, t_ref, hb, he,
     zs, zr, xs, xr, ys, yr, rs, rr, hds, hdr, fs, fr, qs, qr
 ):
     hi = n // PLANE
@@ -64,8 +64,8 @@
     pos = lax.axis_index("frame")
     lox, loy = xnb % PLANE, ynb % PLANE
     ring = [(p + n - 1) % n, (p + 1) % n]
-    bs = (b0, b1, b2)
-    vs = b0.shape[0]
+    bs = [b_ref.at[c] for c in range(3)]
+    vs = b_ref.shape[1]
     ff = x_ref.shape[1]
     hs = sel_ref.shape[1] // 4
 
@@ -128,9 +128,9 @@
 
     def relay(j):
         hh = (h + hi - j) % hi
-        (yc if j % 2 else xc)[j].wait_recv()
-        part = rows(hh, loy if j % 2 else lox)
-        rc[j] = send(part, part, rs.at[j], rr.at[j], xnb if j % 2 else ynb)
+        xc[j].wait_recv()
+        part = rows(hh, lox)
+        rc[j] = send(part, part, rs.at[j], rr.at[j], ynb)
         rc[j].start()
 
     last = 0
@@ -150,7 +150,7 @@
     relay(last)
     halo(2)
     for j in range(hi):
-        (xc if j % 2 else yc)[j].wait_recv()
+        yc[j].wait_recv()
         rc[j].wait_recv()
     swap(0)
     for c in range(3):
@@ -175,10 +175,10 @@
         rc[j].wait_send()
 
 
-def gather_all(x, bases, sel, rsend, n):
+def gather_all(x, basis, sel, rsend, n):
     w, f = x.shape
     hi = n // PLANE
-    vs, kk = bases[0].shape
+    _, vs, kk = basis.shape
     slots = sel.shape[1]
     vm = pl.BlockSpec(memory_space=pltpu.VMEM)
     return pl.pallas_call(
@@ -188,18 +188,18 @@
             jax.ShapeDtypeStruct((vs + slots, 3 * f), x.dtype),
             jax.ShapeDtypeStruct(rsend.shape, rsend.dtype),
         ],
-        in_specs=[vm] * 6,
+        in_specs=[vm] * 4,
         out_specs=[vm] * 3,
         scratch_shapes=[pltpu.VMEM((3, slots, kk), x.dtype)] * 2
         + [DMA((hi,))] * 8 + [DMA((6,))] * 4 + [DMA((2,))] * 2,
         compiler_params=pltpu.CompilerParams(
-            collective_id=0, has_side_effects=True, vmem_limit_bytes=60000 * 1024
+            collective_id=0, has_side_effects=True, vmem_limit_bytes=16000 * 1024
         ),
-    )(x, *bases, sel, rsend)
+    )(x, basis, sel, rsend)
 
 
 def tail_kernel(
-    n, w, own_ref, gh_ref, sel_ref, b0, b1, b2, lt_ref, lo_ref, bg_ref, o_ref,
+    n, w, own_ref, gh_ref, sel_ref, b_ref, lt_ref, lo_ref, bg_ref, o_ref,
     bt, bk, adj, got, acc, g, rl, sb, cx, cy, zb, zl,
     ks, kr, ps, pr, ls, lr, xs, xr, ys, yr, zs, zr,
 ):
@@ -209,8 +209,8 @@
     lox, loy = xnb % PLANE, ynb % PLANE
     lod = PLANE - 1 - lo
     ring = [(p + n - 1) % n, (p + 1) % n]
-    bs = (b0, b1, b2)
-    vs, kk = b0.shape
+    bs = [b_ref.at[c] for c in range(3)]
+    _, vs, kk = b_ref.shape
     ff = lt_ref.shape[1]
     halo = gh_ref.shape[0] // 2
     half = vs // 2
@@ -258,17 +258,14 @@
     def grad(c):
         mine = adj[c, pl.ds(pl.multiple_of(pos * half, half), half)]
         for r in range(0, kk, tile):
-            one = mm(mine, lt_ref[r : r + tile], ((1,), (1,))).astype(BF).astype(F32)
-            two = mm(got[c], lo_ref[r : r + tile], ((1,), (1,))).astype(BF).astype(F32)
-            bg_ref[c, :, r : r + tile] = one + two
+            bg_ref[0, c, :, r : r + tile] = mm(mine, lt_ref[r : r + tile], ((1,), (1,))).astype(BF)
+            bg_ref[1, c, :, r : r + tile] = mm(got[c], lo_ref[r : r + tile], ((1,), (1,))).astype(BF)
 
     order = sorted(range(1, hi), key=lambda j: -min(j, hi - j))
-    even = [j for j in order if j % 2 == 0]
-    odd = [j for j in order if j % 2]
     lc, xc, yc, zc = {}, {}, {}, {}
 
     def via(j):
-        lc[j] = send(rows(j, lod), rl.at[j], ls.at[j], lr.at[j], ynb if j % 2 else xnb)
+        lc[j] = send(rows(j, lod), rl.at[j], ls.at[j], lr.at[j], ynb)
         lc[j].start()
 
     def to_x(j, src):
@@ -281,32 +278,25 @@
 
     def summed(j):
         lc[j].wait_recv()
-        own = rows(j, lox if j % 2 else loy)
+        own = rows(j, lox)
         sb[j] = (own[...].astype(F32) + rl[j].astype(F32)).astype(BF)
-        (to_x if j % 2 else to_y)(j, sb.at[j])
+        to_x(j, sb.at[j])
 
     def total(j):
         xc[j].wait_recv()
         yc[j].wait_recv()
         return rows(j, lo)[...].astype(F32) + cx[j].astype(F32) + cy[j].astype(F32)
 
-    for j in even:
+    for j in order:
         via(j)
-    for j in odd:
-        via(j)
-    for j in even:
-        to_x(j, rows(j, lox))
+        to_y(j, rows(j, loy))
     for c in range(3):
         pc[c].wait_recv()
     grad(0)
-    for j in even:
-        summed(j)
-    for j in odd:
-        to_y(j, rows(j, loy))
-    for j in odd:
+    for j in order:
         summed(j)
     via(0)
-    to_x(0, rows(0, lox))
+    to_y(0, rows(0, loy))
     grad(1)
     for j in order:
         zb[j] = total(j).astype(BF)
@@ -331,7 +321,7 @@
             zc[j].wait_send()
 
 
-def tail(own, gh, sel, bases, lat_t, lat_o, n):
+def tail(own, gh, sel, basis, lat_t, lat_o, n):
     kk, f = lat_t.shape
     w = kk // n
     hi = n // PLANE
@@ -341,10 +331,10 @@
     return pl.pallas_call(
         functools.partial(tail_kernel, n, w),
         out_shape=[
-            jax.ShapeDtypeStruct((3, vs // 2, kk), F32),
+            jax.ShapeDtypeStruct((2, 3, vs // 2, kk), BF),
             jax.ShapeDtypeStruct((w, f), F32),
         ],
-        in_specs=[vm] * 8,
+        in_specs=[vm] * 6,
         out_specs=[vm] * 2,
         scratch_shapes=[
             vmem((3, kk, vs), BF),
@@ -359,9 +349,9 @@
         + [DMA((3,))] * 2
         + [DMA((hi,))] * 8,
         compiler_params=pltpu.CompilerParams(
-            collective_id=1, has_side_effects=True, vmem_limit_bytes=60000 * 1024
+            collective_id=1, has_side_effects=True, vmem_limit_bytes=24000 * 1024
         ),
-    )(own, gh, sel, *bases, lat_t, lat_o)
+    )(own, gh, sel, basis, lat_t, lat_o)
 
 
 def local(basis, latents, rest_pos, triangles, hinges, rest_sq, bend_rest, masses, send_rows):
@@ -379,9 +369,8 @@
     self32 = hot(vs, send_rows.reshape(-1))
     sel = self32.astype(BF)
     rest_out = exact(rest_pos, self32)
-    bases = [basis[c] for c in range(3)]
     rsend = jnp.pad(rest_out.reshape(3, 2, halo).transpose(1, 0, 2), ((0, 0), (0, 5), (0, 0)))
-    lat_t, dext, rhalo = gather_all(latents.T, bases, sel, rsend, n)
+    lat_t, dext, rhalo = gather_all(latents.T, basis, sel, rsend, n)
     lat_o = lax.ppermute(lat_t, "frame", [(0, 1), (1, 0)])
     rest_ext = jnp.concatenate([rest_pos, rhalo[0, :3], rhalo[1, :3]], axis=1)
     rest_edge = exact(rest_ext, inc.astype(F32))
@@ -404,8 +393,8 @@
     g = mm(inc, forces, ((1,), (0,)))
     gh = g[vs:].astype(BF)
     owned = g[:vs].at[:, 2 * ff :].add((GRAVITY / total) * masses[:, None])
-    basis_grad, lg = tail(owned, gh, sel, bases, lat_t, lat_o, n)
-    return (basis_grad, lg.T)
+    halves, lg = tail(owned, gh, sel, basis, lat_t, lat_o, n)
+    return (halves[0].astype(F32) + halves[1].astype(F32), lg.T)
 
 
 def solution(mesh):

time: 102 us -> 95 us (0.931)
  local copies, waits for them, and re-layouts: 10.8 us -> 5.97 us
  Pallas kernels: 78.9 us -> 74.8 us
  other arithmetic: 4.87 us -> 6.34 us
    pallas_call x1, Pallas kernels: 38.9 us -> 34.6 us  [gather_all(): pl.pallas_call(functools.partial(gather_kernel, n, w), out_shape=[jax.Sha...]
    squeeze x1 -> x0, local copies, waits for them, and re-layouts: 2.58 us -> none  [local(): bases = [basis[c] for c in range(3)]]
    unnamed x24 -> x15, local copies, waits for them, and re-layouts: 5.58 us -> 4.03 us
    add x0 -> x1, other arithmetic: none -> 1.44 us  [local(): return (halves[0].astype(F32) + halves[1].astype(F32), lg.T)]
  transfers between devices with their start and end apart: 1 -> 1, of which waited for: 0 -> 0; matrix products, arithmetic and copies ran while one was open for 12% -> 13% of each run, Pallas kernels for 0% -> 0%
where the time goes in v1:
time: 95 us; the launch traced here: 94.6 us
  Pallas kernels  74.8 us (79%)
  matrix products  6.57 us (7%)
  other arithmetic  6.34 us (7%)
  local copies, waits for them, and re-layouts  5.97 us (6%)
    pallas_call x1, Pallas kernels, tail(): pl.pallas_call(functools.partial(tail_kernel, n, w), out_shape=[jax.Shape...  40.1 us
    pallas_call x1, Pallas kernels, gather_all(): pl.pallas_call(functools.partial(gather_kernel, n, w), out_shape=[jax.Sha...  34.6 us
    dot_general x2, matrix products, mm(): return lax.dot_general(a, b, (dims, ((), ())), preferred_element_type=F32)  5.05 us
    unnamed x15, local copies, waits for them, and re-layouts  4.03 us
    another operation x6, other arithmetic  3.85 us
  transfers between devices with their start and end apart: 1, of which 0 were waited for; matrix products, arithmetic and copies ran while one was open for 13% of the time, Pallas kernels for 0%

profile of v1, /device:TPU:0, one launch (start us, length us, event | category | flops | bytes accessed | tf_op | source)
XLA Modules:
  0.0 94.6 jit_solution(783420895880761217)
XLA Ops:
  0.6 0.0 copy-start.6
  0.6 0.7 convert_convert_fusion.sel_ref
  1.4 0.9 convolution_bitcast_fusion
  2.2 0.0 copy-start
  2.3 1.4 %copy-done = bf16[3,256,1024]{2,1,0:T(8,128)(2,1)S(1)} copy-done((bf16[3,256,1024]{2,1,0:T(8,128)(2,1)S(1)}, bf16[3,256,1024]{2,1,0:T(8,128)(2,1)}, u32[]{:S(2)}) %copy-start) | copy-done | bytes 1572888
  3.7 0.0 copy-start.2
  3.7 0.8 copy-done.2
  4.5 34.6 %shard_map.104 = (bf16[1024,512]{1,0:T(8,128)(2,1)S(1)}, bf16[512,1536]{1,0:T(8,128)(2,1)S(1)}, f32[2,8,128]{2,1,0:T(8,128)S(1)}) custom-call(bf16[64,512]{1,0:T(8,128)(2,1)S(1)} %bitcast.30, bf16[3,256,1024]{2,1,0:T(8,128)(2,1)S(1)} %copy-done, bf16[256,256]{1,0:T(8,128)(2,1)S(1)} %convert_convert_fusion.sel_ref, f32[2,8,128]{2,1,0:T(8,128)S(1)} %pad.8.r_ref), custom_call_target="tpu_custom_call" | custom-call | tf_op jit(solution)/shard_map/pallas_call | solution.py:184
  39.1 0.1 collective-permute-start
  39.3 0.9 slice_reduce_fusion.6
  40.1 0.8 fusion.36
  40.9 0.4 fusion.15
  41.4 0.4 subtract_convert_fusion.6
  41.8 0.0 copy-done.6
  41.8 0.7 fusion.22
  42.5 0.0 copy-start.4
  42.5 0.0 copy-start.3
  42.5 2.5 %fusion.30 = f32[1408,1536]{1,0:T(8,128)S(1)} fusion(bf16[512,1536]{1,0:T(8,128)(2,1)S(1)} %get-tuple-element.31, bf16[512,384]{1,0:T(8,128)(2,1)S(1)} %subtract_convert_fusion.6, bf16[512,512]{1,0:T(8,128)(2,1)S(1)} %get-tuple-element.73, bf16[512,512]{1,0:T(8,128)(2,1)S(1)} %get-tuple-element.72), kind=kOutput, calls=%fused_computation.80 | convolution fusion | flops 2218917888 | bytes 11665408 | tf_op jit(solution)/shard_map/dot_general | solution.py:23
  45.0 0.0 copy-done.4
  45.0 0.0 copy-done.3
  45.0 1.4 %subtract_convert_fusion.5 = (bf16[512,512]{1,0:T(8,128)(2,1)S(1)}, f32[512,512]{1,0:T(8,128)S(1)}, f32[512,512]{1,0:T(8,128)S(1)}, f32[512,512]{1,0:T(8,128)S(1...) fusion(f32[1408,1536]{1,0:T(8,128)S(1)} %fusion.30, f32[512]{0:T(512)S(1)} %bitcast.43, f32[512]{0:T(512)S(1)} %bitcast.45, ...), kind=kLoop, calls=%fused_computation.38 | loop fusion | flops 7340032 | bytes 12075008 | tf_op jit(solution)/shard_map/convert.7
  46.5 0.6 subtract_convert_fusion.2
  47.1 0.2 slice_add_fusion.8
  47.3 0.1 fusion.14
  47.5 0.8 subtract_convert_fusion.4
  48.3 2.6 %fusion = f32[512,1536]{1,0:T(8,128)S(1)} fusion(bf16[384,1536]{1,0:T(8,128)(2,1)S(1)} %fusion.14, bf16[512,512]{1,0:T(8,128)(2,1)S(1)} %get-tuple-element.53, bf16[512,512]{1,0:T(8,128)(2,1)S(1)} %get-tuple-element.52, bf16[512,512]{1,0:T(8,128)(2,1)S(1)} %get-tuple-element.49, bf16[512,512]{1,0:T(8,128)(2,1)S(1)} %get-tuple-element.54, ...), kind=kOutput, calls=%fused_computation | convolution fusion | flops 2249195520 | bytes 8912896 | tf_op jit(solution)/shard_map/dot_general | solution.py:23
  50.9 0.0 copy-start.5
  50.9 0.0 copy-start.1
  50.9 0.1 slice.200
  51.1 0.1 slice.264.gh_ref
  51.1 0.5 copy-done.5
  51.6 0.1 fusion.20.own_ref
  51.7 0.0 collective-permute-done.lo_ref
  51.7 0.6 copy-done.1
  52.3 40.1 %shard_map.105 = (bf16[2,3,128,1024]{3,2,1,0:T(8,128)(2,1)S(1)}, f32[64,512]{1,0:T(8,128)S(1)}) custom-call(f32[256,1536]{1,0:T(8,128)S(1)} %fusion.20.own_ref, bf16[256,1536]{1,0:T(8,128)(2,1)S(1)} %slice.264.gh_ref, bf16[256,256]{1,0:T(8,128)(2,1)S(1)} %convert_convert_fusion.sel_ref, bf16[3,256,1024]{2,1,0:T(8,128)(2,1)S(1)} %copy-done.1, ...), custom_call_target="tpu_custom_call" | custom-call | tf_op jit(solution)/shard_map/pallas_call | solution.py:331
  92.5 1.4 %add_bitcast_fusion = f32[3,128,1024]{2,1,0:T(8,128)} fusion(bf16[2,3,128,1024]{3,2,1,0:T(8,128)(2,1)S(1)} %get-tuple-element.34), kind=kLoop, calls=%fused_computation.17 | loop fusion | flops 1179648 | bytes 3145728 | tf_op jit(solution)/shard_map/add | solution.py:397
  93.9 0.7 copy.13
  (7 shorter events, 0.1 us)
Async XLA Ops:
  0.6 41.1 %copy-start.6 = (f32[3,256]{1,0:T(4,128)S(1)}, f32[3,256]{1,0:T(4,128)}, u32[]{:S(2)}) copy-start(f32[3,256]{1,0:T(4,128)} %param.15) | copy-start | bytes 9220
  2.2 1.4 %copy-start = (bf16[3,256,1024]{2,1,0:T(8,128)(2,1)S(1)}, bf16[3,256,1024]{2,1,0:T(8,128)(2,1)}, u32[]{:S(2)}) copy-start(bf16[3,256,1024]{2,1,0:T(8,128)(2,1)} %b_ref.3) | copy-start | bytes 4718596
  3.7 0.8 copy-start.2
  39.1 12.6 %collective-permute-start = (bf16[1024,512]{1,0:T(8,128)(2,1)S(1)}, bf16[1024,512]{1,0:T(8,128)(2,1)S(1)}, u32[]{:S(2)}, u32[]{:S(2)}) collective-permute-start(bf16[1024,512]{1,0:T(8,128)(2,1)S(1)} %get-tuple-element.33.lt_ref), channel_id=1, source_target_pairs={{0,1},{1,0},{2,3},{3,2},{4,5},{5,4},{6,7},{7,6},{8,9},{9,8},{10,11... | collective-permute-start | bytes 3145736 | tf_op jit(solution)/shard_map/ppermute | solution.py:374
  42.5 2.5 %copy-start.4 = (f32[3,512]{1,0:T(4,128)S(1)}, f32[3,512]{1,0:T(4,128)}, u32[]{:S(2)}) copy-start(f32[3,512]{1,0:T(4,128)} %param.18) | copy-start | bytes 18436
  42.5 2.5 %copy-start.3 = (f32[3,384]{1,0:T(4,128)S(1)}, f32[3,384]{1,0:T(4,128)}, u32[]{:S(2)}) copy-start(f32[3,384]{1,0:T(4,128)} %param.19) | copy-start | bytes 13828
  50.9 0.7 copy-start.5
  50.9 1.4 %copy-start.1 = (bf16[3,256,1024]{2,1,0:T(8,128)(2,1)S(1)}, bf16[3,256,1024]{2,1,0:T(8,128)(2,1)}, u32[]{:S(2)}) copy-start(bf16[3,256,1024]{2,1,0:T(8,128)(2,1)} %b_ref.3) | copy-start | bytes 4718596

commit v2 on v1

v2 whole, which is shorter than its diff:
```python
import functools

import jax
import jax.numpy as jnp
from jax import lax
from jax.experimental import pallas as pl
from jax.experimental.pallas import tpu as pltpu
from jax.sharding import PartitionSpec as P

MEMBRANE = 5.0
BENDING = 5.0
GRAVITY = 40.0
BF = jnp.bfloat16
F32 = jnp.float32
PLANE = 4
LANES = 128
CHUNKS = 2
MESH_ID = pl.DeviceIdType.MESH
DMA = pltpu.SemaphoreType.DMA


def mm(a, b, dims=((1,), (0,))):
    return lax.dot_general(a, b, (dims, ((), ())), preferred_element_type=F32)


NT = ((1,), (1,))
TN = ((0,), (0,))


def split3(r):
    hi = r.astype(BF)
    left = r - hi.astype(F32)
    mid = left.astype(BF)
    return hi, mid, (left - mid.astype(F32)).astype(BF)


def send(src, dst, ss, rs, q):
    return pltpu.make_async_remote_copy(
        src_ref=src, dst_ref=dst, send_sem=ss, recv_sem=rs,
        device_id={"patch": q}, device_id_type=MESH_ID,
    )


def column(row):
    return jnp.broadcast_to(row, (LANES, row.shape[1])).T


def kernel(
    n, frames,
    x_hbm, b_hbm, rest_hbm, tri_hbm, hin_hbm, rsq_hbm, bend_hbm, mass_hbm, rows_hbm,
    bg_ref, lg_ref,
    xs, xo, be, bet, hb, tri, hin, rsq, bend, mass, rows, restb, restx, sel, inc, inct,
    rb, sq, bd, mb, dec, edge, force, adj, own, bk, tot, got, g, yl, ysum, zl, xsum, xl,
    ins, xsem, ysem, zsem, rsem, hsem, wsem, osem, ksem, psem, ry, rz, rx,
):
    hi = n // PLANE
    w = x_hbm.shape[0]
    p = lax.axis_index("patch")
    pos = lax.axis_index("frame")
    h, lo = p // PLANE, p % PLANE
    xnb = p + 1 - 2 * (p % 2)
    ynb = p + 2 - 4 * ((p // 2) % 2)
    lox, loy, lod = xnb % PLANE, ynb % PLANE, PLANE - 1 - lo
    ring = [(p + n - 1) % n, (p + 1) % n]
    vs, kk = b_hbm.shape[1:]
    ff = x_hbm.shape[1]
    halo = rows_hbm.shape[1]
    ext = vs + 2 * halo
    hs = halo // 2
    nt, nh = tri_hbm.shape[1], hin_hbm.shape[1]
    half = vs // 2
    pc = ff // CHUNKS
    tile = 256

    def partner(src, dst, sems, at):
        return pltpu.make_async_remote_copy(
            src_ref=src, dst_ref=dst, send_sem=sems.at[0, at], recv_sem=sems.at[1, at],
            device_id={"frame": 1 - pos}, device_id_type=MESH_ID,
        )

    out = []

    def go(src, dst, sems, at, q):
        c = send(src, dst, sems.at[0, at], sems.at[1, at], q)
        c.start()
        out.append(c)
        return c

    def cross(src, dst, sems, at):
        c = partner(src, dst, sems, at)
        c.start()
        out.append(c)
        return c

    small = [(rows_hbm, rows), (rest_hbm, restb), (tri_hbm, tri), (hin_hbm, hin),
             (rsq_hbm, rsq), (bend_hbm, bend), (mass_hbm, mass)]
    ends = [(s, d) for s, d in small[:2]]
    ends += [(b_hbm.at[c], be.at[c, pl.ds(0, vs)]) for c in range(3)]
    ends += small[2:]
    fetch = [pltpu.make_async_copy(s, d, ins.at[i]) for i, (s, d) in enumerate(ends)]
    for f in fetch:
        f.start()

    zpeer = [((h + j) % hi) * PLANE + lo for j in range(hi)]

    def row(hh, ll):
        return xs.at[pl.ds(pl.multiple_of((hh * PLANE + ll) * w, w), w)]

    mine = row(h, lo)
    keep = pltpu.make_async_copy(x_hbm, mine, ins.at[len(ends)])
    keep.start()

    bar = pltpu.get_barrier_semaphore()
    pl.semaphore_signal(bar, inc=1, device_id={"frame": 1 - pos}, device_id_type=MESH_ID)
    peers = zpeer[1:] + [xnb, ynb] + ring
    for q in peers:
        pl.semaphore_signal(bar, inc=1, device_id={"patch": q}, device_id_type=MESH_ID)
    pl.semaphore_wait(bar, len(peers) + 1)

    order = sorted(range(1, hi), key=lambda j: -min(j, hi - j))
    near = order[::-1]
    xc = go(x_hbm, mine, xsem, 0, xnb)
    za, zb, ya, yb = {}, {}, {}, {}
    for j in order:
        za[j] = go(x_hbm, mine, zsem, j, zpeer[j])
    ya[0] = go(x_hbm, mine, ysem, 0, ynb)

    def hot(count, ids, dtype):
        iota = lax.broadcasted_iota(jnp.int32, (count, ids.shape[1]), 0)
        return jnp.where(iota == ids, 1.0, 0.0).astype(dtype)

    fetch[0].wait()
    fetch[1].wait()
    for d in range(2):
        sel[:, d * halo : (d + 1) * halo] = hot(vs, rows[d : d + 1], BF)
    parts = split3(restb[...])
    sent = sum(mm(part, sel[...]) for part in parts)
    rc = []
    for d in range(2):
        restx[d] = sent[:, d * halo : (d + 1) * halo]
        rc.append(go(restx.at[d], restx.at[3 - d], rsem, d, ring[d]))

    hc, fc = {}, {}

    def part_of(ref, base, c, d):
        at = pl.multiple_of(base + d * halo + pos * hs, hs)
        return ref.at[c, pl.ds(at, hs)]

    for c in range(3):
        fetch[2 + c].wait()
        hb[c] = mm(sel[...], be[c, 0:vs], TN).astype(BF)
        for d in range(2):
            hc[c, d] = go(
                part_of(hb, 0, c, d), part_of(be, vs, c, 1 - d), hsem, 2 * c + d, ring[d]
            )
        if c == 0:
            xc.wait_recv()
            side = row(h, lox)
            for j in order:
                zb[j] = go(side, side, zsem, hi + j, zpeer[j])
            yb[0] = go(side, side, ysem, hi, ynb)

    def relay(j):
        hh = (h + hi - j) % hi
        za[j].wait_recv()
        part = row(hh, lo)
        ya[j] = go(part, part, ysem, j, ynb)

    def relay_side(j):
        hh = (h + hi - j) % hi
        zb[j].wait_recv()
        part = row(hh, lox)
        yb[j] = go(part, part, ysem, hi + j, ynb)

    def swap(c):
        for d in range(2):
            hc[c, d].wait_recv()
            part = part_of(be, vs, c, 1 - d)
            fc[c, d] = cross(part, part, wsem, 2 * c + d)

    for f in fetch[5:]:
        f.wait()

    def corner(ref, i, at, count):
        return hot(ext, ref[i : i + 1, at : at + count], F32)

    def build(at, count, plus, minus):
        total = None
        for ref, i, begin in plus:
            one = corner(ref, i, begin, count)
            total = one if total is None else total + one
        for ref, i, begin in minus:
            total = total - corner(ref, i, begin, count)
        inc[:, at : at + count] = total.astype(BF)
        inct[at : at + count] = inc[:, at : at + count].T

    def build_edges(i):
        for b in range(0, nt, LANES):
            build(i * nt + b, LANES, [(tri, i + 1, b)], [(tri, i, b)])

    for j in near:
        relay(j)
    build_edges(0)
    for j in near:
        relay_side(j)
    build_edges(1)
    for b in range(0, nh, LANES):
        build(
            2 * nt + b, LANES, [(hin, 2, b), (hin, 3, b)], [(hin, 0, b), (hin, 1, b)]
        )
    swap(0)
    keep.wait()

    for i in range(3):
        sq[i] = column(rsq[i : i + 1])
        bd[i] = column(bend[i : i + 1])
    mb[...] = column(mass[...])
    for d in range(2):
        rc[d].wait_recv()
    for c in range(3):
        line = jnp.concatenate(
            [restb[c : c + 1], restx[2, c : c + 1], restx[3, c : c + 1]], axis=1
        )
        cols = sum(
            mm(inct[...], jnp.broadcast_to(part, (LANES, ext)), NT) for part in split3(line)
        )
        rb[c, 0 : 2 * nt] = cols[0 : 2 * nt]
        rb[c, 2 * nt :] = cols[2 * nt :] - bd[c]
    for c in range(3):
        bet[:, c * ext : c * ext + vs] = be[c, 0:vs].T

    for j in range(hi):
        ya[j].wait_recv()
        yb[j].wait_recv()

    def decode(c, at, count, lanes):
        dec[c, at : at + count, lanes] = mm(be[c, at : at + count], xs[:, lanes]).astype(BF)

    def stretch(c, lanes):
        for r in range(0, 2 * nt + nh, 352):
            edge[c, r : r + 352, lanes] = mm(inct[r : r + 352], dec[c, :, lanes])

    every = pl.ds(0, ff)
    for c in range(3):
        decode(c, 0, vs, every)
        if c == 0:
            swap(1)
    for c in range(2):
        for d in range(2):
            fc[c, d].wait_recv()
        decode(c, vs, 2 * halo, every)
        stretch(c, every)
        bet[:, c * ext + vs : (c + 1) * ext] = be[c, vs:ext].T
    swap(2)
    oc = cross(xs, xo, osem, 0)
    for d in range(2):
        fc[2, d].wait_recv()

    k = 4.0 * MEMBRANE / frames
    kc, yc, pcs = {}, {}, {}

    def elastic(q):
        step = 16

        def body(i, carry):
            r = pl.multiple_of(i * step, step)
            for t in range(0, pc, LANES):
                lanes = pl.ds(q * pc + t, LANES)
                e1 = [edge[c, pl.ds(r, step), lanes] + rb[c, pl.ds(r, step)] for c in range(3)]
                r2 = pl.multiple_of(nt + r, step)
                e2 = [edge[c, pl.ds(r2, step), lanes] + rb[c, pl.ds(r2, step)] for c in range(3)]
                e3 = [a + b for a, b in zip(e1, e2)]

                def strain(e, i):
                    return e[0] * e[0] + e[1] * e[1] + e[2] * e[2] - sq[i, pl.ds(r, step)]

                s1, s2, s3 = strain(e1, 0), strain(e2, 1), strain(e3, 2)
                for c in range(3):
                    u = s3 * e3[c]
                    force[c, pl.ds(r, step), pl.ds(t, LANES)] = (s1 * e1[c] + u).astype(BF)
                    force[c, pl.ds(r2, step), pl.ds(t, LANES)] = (s2 * e2[c] + u).astype(BF)
            return carry

        lax.fori_loop(0, nt // step, body, 0)

        def bend_body(i, carry):
            r = pl.multiple_of(2 * nt + i * step, step)
            for c in range(3):
                for t in range(0, pc, LANES):
                    e = edge[c, pl.ds(r, step), pl.ds(q * pc + t, LANES)] + rb[c, pl.ds(r, step)]
                    force[c, pl.ds(r, step), pl.ds(t, LANES)] = (
                        e * (0.5 * BENDING / MEMBRANE)
                    ).astype(BF)
            return carry

        lax.fori_loop(0, nh // step, bend_body, 0)

    for q in range(CHUNKS):
        lanes = pl.ds(q * pc, pc)
        decode(2, vs, 2 * halo, lanes)
        stretch(2, lanes)
        elastic(q)
        for c in range(3):
            adj[q, c * ext + vs : (c + 1) * ext] = (mm(inc[vs:ext], force[c]) * k).astype(BF)
            for d in range(2):
                kc[q, c, d] = go(
                    adj.at[q, pl.ds(c * ext + vs + d * halo, halo)],
                    bk.at[q, c, pl.ds((1 - d) * halo, halo)],
                    ksem, (q * 3 + c) * 2 + d, ring[d],
                )
        for c in range(3):
            part = mm(inc[0:vs], force[c]) * k
            if c == 2:
                lift = mb[...] * (GRAVITY / frames)
                part = part + jnp.concatenate([lift] * (pc // LANES), axis=1)
            own[q, c] = part
            adj[q, c * ext : c * ext + vs] = part.astype(BF)
        if q == 0:
            bet[:, 2 * ext + vs : 3 * ext] = be[2, vs:ext].T
        for r in range(0, kk, tile):
            g[q, r : r + tile] = mm(bet[r : r + tile], adj[q]).astype(BF)
        for j in order + [0]:
            hh = (h + j) % hi
            for i, ll in enumerate((loy, lod)):
                at = pl.multiple_of((hh * PLANE + ll) * w, w)
                yc[q, j, i] = go(
                    g.at[q, pl.ds(at, w)], yl.at[q, j, i], ry, (q * hi + j) * 2 + i, ynb
                )

    def fold(q, j, i):
        hh = (h + j) % hi
        at = pl.multiple_of((hh * PLANE + (lox if i else lo)) * w, w)
        yc[q, j, i].wait_recv()
        return g[q, pl.ds(at, w)].astype(F32) + yl[q, j, i].astype(F32)

    zc = {}

    def depth(q):
        for j in order:
            for i in range(2):
                ysum[q, j, i] = fold(q, j, i).astype(BF)
                zc[q, j, i] = go(
                    ysum.at[q, j, i], zl.at[q, j, i], rz, (q * hi + j) * 2 + i, zpeer[j]
                )

    held = {}

    def gather_z(q, i):
        s = fold(q, 0, i)
        for j in order:
            zc[q, j, i].wait_recv()
            s = s + zl[q, j, i].astype(F32)
        return s

    def collect(q):
        for c in range(3):
            kc[q, c, 0].wait_recv()
            kc[q, c, 1].wait_recv()
            tot[c, :, q * pc : (q + 1) * pc] = (own[q, c] + mm(sel[...], bk[q, c])).astype(BF)
            theirs = pl.ds(pl.multiple_of((1 - pos) * half, half), half)
            pcs[q, c] = cross(
                tot.at[c, theirs, pl.ds(q * pc, pc)], got.at[c, :, pl.ds(q * pc, pc)],
                psem, q * 3 + c,
            )

    rxc = {}

    def turn(q):
        xsum[q] = gather_z(q, 1).astype(BF)
        rxc[q] = go(xsum.at[q], xl.at[q], rx, q, xnb)

    def finish(q):
        s = gather_z(q, 0)
        rxc[q].wait_recv()
        lg_ref[:, q * pc : (q + 1) * pc] = s + xl[q].astype(F32)

    def product(which, src, lat, c):
        for r in range(0, kk, tile):
            bg_ref[which, c, :, r : r + tile] = mm(src, lat[r : r + tile], NT).astype(BF)

    for q in range(CHUNKS):
        depth(q)
    for q in range(CHUNKS - 1):
        collect(q)
    for q in range(CHUNKS):
        turn(q)
    collect(CHUNKS - 1)
    for c in range(3):
        product(0, tot[c, pl.ds(pl.multiple_of(pos * half, half), half)], xs, c)
    oc.wait_recv()
    for c in range(3):
        for q in range(CHUNKS):
            pcs[q, c].wait_recv()
        product(1, got[c], xo, c)
    for q in range(CHUNKS):
        finish(q)
    for c in out:
        c.wait_send()


def local(basis, latents, rest_pos, triangles, hinges, rest_sq, bend_rest, masses, send_rows):
    vs, kk = basis.shape[1:]
    ff, w = latents.shape
    halo = send_rows.shape[1]
    nt, nh = triangles.shape[1], hinges.shape[1]
    n = lax.axis_size("patch")
    hi = n // PLANE
    frames = ff * lax.axis_size("frame")
    ext = vs + 2 * halo
    ne = 2 * nt + nh
    pc = ff // CHUNKS
    v = pltpu.VMEM
    i32 = jnp.int32
    vm = pl.BlockSpec(memory_space=pltpu.VMEM)
    hbm = pl.BlockSpec(memory_space=pltpu.HBM)
    halves, lg = pl.pallas_call(
        functools.partial(kernel, n, frames),
        out_shape=[
            jax.ShapeDtypeStruct((2, 3, vs // 2, kk), BF),
            jax.ShapeDtypeStruct((w, ff), F32),
        ],
        in_specs=[hbm] * 9,
        out_specs=[vm] * 2,
        scratch_shapes=[
            v((kk, ff), BF),
            v((kk, ff), BF),
            v((3, ext, kk), BF),
            v((kk, 3 * ext), BF),
            v((3, 2 * halo, kk), BF),
            v((3, nt), i32),
            v((4, nh), i32),
            v((3, nt), F32),
            v((3, nh), F32),
            v((1, vs), F32),
            v((2, halo), i32),
            v((3, vs), F32),
            v((4, 3, halo), F32),
            v((vs, 2 * halo), BF),
            v((ext, ne), BF),
            v((ne, ext), BF),
            v((3, ne, LANES), F32),
            v((3, nt, LANES), F32),
            v((3, nh, LANES), F32),
            v((vs, LANES), F32),
            v((3, ext, ff), BF),
            v((3, ne, ff), F32),
            v((3, ne, pc), BF),
            v((CHUNKS, 3 * ext, pc), BF),
            v((CHUNKS, 3, vs, pc), F32),
            v((CHUNKS, 3, 2 * halo, pc), BF),
            v((3, vs, ff), BF),
            v((3, vs // 2, ff), BF),
            v((CHUNKS, kk, pc), BF),
            v((CHUNKS, hi, 2, w, pc), BF),
            v((CHUNKS, hi, 2, w, pc), BF),
            v((CHUNKS, hi, 2, w, pc), BF),
            v((CHUNKS, w, pc), BF),
            v((CHUNKS, w, pc), BF),
            DMA((11,)),
            DMA((2, 1)),
            DMA((2, 2 * hi)),
            DMA((2, 2 * hi)),
            DMA((2, 2)),
            DMA((2, 6)),
            DMA((2, 6)),
            DMA((2, 1)),
            DMA((2, CHUNKS * 6)),
            DMA((2, CHUNKS * 3)),
            DMA((2, CHUNKS * hi * 2)),
            DMA((2, CHUNKS * hi * 2)),
            DMA((2, CHUNKS)),
        ],
        compiler_params=pltpu.CompilerParams(
            collective_id=0, has_side_effects=True, vmem_limit_bytes=52000 * 1024
        ),
    )(
        latents.T, basis, rest_pos, triangles, hinges, rest_sq, bend_rest,
        masses.reshape(1, vs), send_rows,
    )
    return (halves[0].astype(F32) + halves[1].astype(F32), lg.T)


def solution(mesh):
    return jax.shard_map(
        local,
        mesh=mesh,
        in_specs=(
            P(None, "patch", None),
            P("frame", "patch"),
            P(None, "patch"),
            P(None, "patch"),
            P(None, "patch"),
            P(None, "patch"),
            P(None, "patch"),
            P("patch"),
            P(None, "patch"),
        ),
        out_specs=(P(None, ("patch", "frame"), None), P("frame", "patch")),
        check_vma=False,
    )
```

time: 95 us -> 77.3 us (0.81)
  matrix products: 6.57 us -> 0 us
  Pallas kernels: 74.8 us -> 68.5 us
  other arithmetic: 6.34 us -> 1.43 us
    dot_general x4 -> x0, matrix products: 6.57 us -> none  [the longest x2 5.05 us: mm(): return lax.dot_general(a, b, (dims, ((), ())), preferred_element_type=F32)]
    pallas_call x2 -> x1, Pallas kernels: 74.8 us -> 68.5 us  [local(): pl.pallas_call(functools.partial(kernel, n, frames), out_shape=[jax.Shape...]
    another operation x6 -> x0, other arithmetic: 3.85 us -> none
    unnamed x15 -> x17, local copies, waits for them, and re-layouts: 4.03 us -> 6.31 us
    slice x7 -> x0, local copies, waits for them, and re-layouts: 1.92 us -> none  [the longest x1 0.87 us: local(): ha, hb, hc, hd = (hot(ext, hinges[i]) for i in range(4))]
  transfers between devices with their start and end apart: 1 -> 0, of which waited for: 0 -> 0; matrix products, arithmetic and copies ran while one was open for 13% -> 0% of each run, Pallas kernels for 0% -> 0%
where the time goes in v2:
time: 77.3 us; the launch traced here: 76.9 us
  Pallas kernels  68.5 us (89%)
  local copies, waits for them, and re-layouts  6.31 us (8%)
  other arithmetic  1.43 us (2%)
    pallas_call x1, Pallas kernels, local(): pl.pallas_call(functools.partial(kernel, n, frames), out_shape=[jax.Shape...  68.5 us
    unnamed x17, local copies, waits for them, and re-layouts  6.31 us

profile of v2, /device:TPU:0, one launch (start us, length us, event | category | flops | bytes accessed | tf_op | source)
XLA Modules:
  0.0 76.9 jit_solution(5385569654025517967)
XLA Ops:
  0.6 0.0 copy-start
  0.6 0.8 %copy-done = bf16[512,64]{0,1:T(8,128)(2,1)S(1)} copy-done((bf16[512,64]{0,1:T(8,128)(2,1)S(1)}, bf16[512,64]{0,1:T(8,128)(2,1)}, u32[]{:S(2)}) %copy-start) | copy-done | bytes 65560
  1.5 0.0 copy-start.1
  1.5 0.7 copy-done.1
  2.2 0.0 copy-start.2
  2.2 0.7 copy-done.2
  2.9 0.0 copy-start.3
  2.9 0.7 copy-done.3
  3.6 0.0 copy-start.4
  3.6 0.7 copy-done.4
  4.3 0.0 copy-start.5
  4.3 0.7 copy-done.5
  4.9 0.0 copy-start.6
  4.9 0.7 copy-done.6
  5.6 0.0 copy-start.7
  5.6 0.7 copy-done.7
  6.3 68.5 %shard_map.104 = (bf16[2,3,128,1024]{3,2,1,0:T(8,128)(2,1)S(1)}, f32[64,512]{1,0:T(8,128)S(1)}) custom-call(bf16[64,512]{1,0:T(8,128)(2,1)S(1)} %bitcast.6, bf16[3,256,1024]{2,1,0:T(8,128)(2,1)} %b_hbm.1, f32[3,256]{1,0:T(4,128)S(1)} %copy-done.5, s32[3,512]{1,0:T(4,128)S(1)} %copy-done.1, s32[4,384]{1,0:T(4,128)S(1)} %copy-done.3, f32[3,512]{1,0:T(4,128)S(1)} %copy-done.2, ...), custom_call_target="tpu_custom_call" | custom-call | tf_op jit(solution)/shard_map/pallas_call | solution.py:416
  74.8 1.4 %add_bitcast_fusion = f32[3,128,1024]{2,1,0:T(8,128)} fusion(bf16[2,3,128,1024]{3,2,1,0:T(8,128)(2,1)S(1)} %get-tuple-element.4), kind=kLoop, calls=%fused_computation | loop fusion | flops 1179648 | bytes 3145728 | tf_op jit(solution)/shard_map/add | solution.py:480
  76.2 0.7 copy.12
Async XLA Ops:
  0.6 0.8 %copy-start = (bf16[512,64]{0,1:T(8,128)(2,1)S(1)}, bf16[512,64]{0,1:T(8,128)(2,1)}, u32[]{:S(2)}) copy-start(bf16[512,64]{0,1:T(8,128)(2,1)} %param.10) | copy-start | bytes 196612
  1.5 0.7 copy-start.1
  2.2 0.7 copy-start.2
  2.9 0.7 copy-start.3
  3.6 0.7 copy-start.4
  4.3 0.7 copy-start.5
  4.9 0.7 copy-start.6
  5.6 0.7 copy-start.7

commit v3 on v2

--- a/solution.py
+++ b/solution.py
@@ -61,6 +61,9 @@
     xnb = p + 1 - 2 * (p % 2)
     ynb = p + 2 - 4 * ((p // 2) % 2)
     lox, loy, lod = xnb % PLANE, ynb % PLANE, PLANE - 1 - lo
+    odd = p % 2
+    toward = [xnb, (p + n - 1 + 2 * odd) % n]
+    slot = [1 - odd, odd]
     ring = [(p + n - 1) % n, (p + 1) % n]
     vs, kk = b_hbm.shape[1:]
     ff = x_hbm.shape[1]
@@ -103,11 +106,16 @@
 
     zpeer = [((h + j) % hi) * PLANE + lo for j in range(hi)]
 
-    def row(hh, ll):
-        return xs.at[pl.ds(pl.multiple_of((hh * PLANE + ll) * w, w), w)]
-
-    mine = row(h, lo)
-    keep = pltpu.make_async_copy(x_hbm, mine, ins.at[len(ends)])
+    def row(hh, ll, q):
+        at = pl.multiple_of((hh * PLANE + ll) * w, w)
+        return xs.at[pl.ds(at, w), pl.ds(q * pc, pc)]
+
+    def source(q):
+        return x_hbm.at[:, pl.ds(q * pc, pc)]
+
+    keep = pltpu.make_async_copy(
+        x_hbm, xs.at[pl.ds(pl.multiple_of(p * w, w), w)], ins.at[len(ends)]
+    )
     keep.start()
 
     bar = pltpu.get_barrier_semaphore()
@@ -119,11 +127,40 @@
 
     order = sorted(range(1, hi), key=lambda j: -min(j, hi - j))
     near = order[::-1]
-    xc = go(x_hbm, mine, xsem, 0, xnb)
-    za, zb, ya, yb = {}, {}, {}, {}
-    for j in order:
-        za[j] = go(x_hbm, mine, zsem, j, zpeer[j])
-    ya[0] = go(x_hbm, mine, ysem, 0, ynb)
+    xc, za, zb, ya, yb = {}, {}, {}, {}, {}
+
+    def open_x(q):
+        xc[q] = go(source(q), row(h, lo, q), xsem, q, xnb)
+
+    def open_rest(q):
+        for j in order:
+            za[q, j] = go(source(q), row(h, lo, q), zsem, 2 * hi * q + j, zpeer[j])
+        ya[q, 0] = go(source(q), row(h, lo, q), ysem, 2 * hi * q, ynb)
+
+    def side(q):
+        xc[q].wait_recv()
+        part = row(h, lox, q)
+        for j in order:
+            zb[q, j] = go(part, part, zsem, 2 * hi * q + hi + j, zpeer[j])
+        yb[q, 0] = go(part, part, ysem, 2 * hi * q + hi, ynb)
+
+    def relay(q, j):
+        za[q, j].wait_recv()
+        part = row((h + hi - j) % hi, lo, q)
+        ya[q, j] = go(part, part, ysem, 2 * hi * q + j, ynb)
+
+    def relay_side(q, j):
+        zb[q, j].wait_recv()
+        part = row((h + hi - j) % hi, lox, q)
+        yb[q, j] = go(part, part, ysem, 2 * hi * q + hi + j, ynb)
+
+    def arrive(q):
+        for j in range(hi):
+            ya[q, j].wait_recv()
+            yb[q, j].wait_recv()
+
+    open_x(0)
+    open_rest(0)
 
     def hot(count, ids, dtype):
         iota = lax.broadcasted_iota(jnp.int32, (count, ids.shape[1]), 0)
@@ -138,7 +175,8 @@
     rc = []
     for d in range(2):
         restx[d] = sent[:, d * halo : (d + 1) * halo]
-        rc.append(go(restx.at[d], restx.at[3 - d], rsem, d, ring[d]))
+    for i in range(2):
+        rc.append(go(restx.at[slot[i]], restx.at[3 - slot[i]], rsem, i, toward[i]))
 
     hc, fc = {}, {}
 
@@ -146,37 +184,26 @@
         at = pl.multiple_of(base + d * halo + pos * hs, hs)
         return ref.at[c, pl.ds(at, hs)]
 
+    def reach(c, i):
+        hc[c, i] = go(
+            part_of(hb, 0, c, slot[i]), part_of(be, vs, c, 1 - slot[i]),
+            hsem, 2 * c + i, toward[i],
+        )
+
     for c in range(3):
         fetch[2 + c].wait()
         hb[c] = mm(sel[...], be[c, 0:vs], TN).astype(BF)
-        for d in range(2):
-            hc[c, d] = go(
-                part_of(hb, 0, c, d), part_of(be, vs, c, 1 - d), hsem, 2 * c + d, ring[d]
-            )
+        reach(c, 1)
+        reach(c, 0)
         if c == 0:
-            xc.wait_recv()
-            side = row(h, lox)
-            for j in order:
-                zb[j] = go(side, side, zsem, hi + j, zpeer[j])
-            yb[0] = go(side, side, ysem, hi, ynb)
-
-    def relay(j):
-        hh = (h + hi - j) % hi
-        za[j].wait_recv()
-        part = row(hh, lo)
-        ya[j] = go(part, part, ysem, j, ynb)
-
-    def relay_side(j):
-        hh = (h + hi - j) % hi
-        zb[j].wait_recv()
-        part = row(hh, lox)
-        yb[j] = go(part, part, ysem, hi + j, ynb)
-
-    def swap(c):
-        for d in range(2):
-            hc[c, d].wait_recv()
-            part = part_of(be, vs, c, 1 - d)
-            fc[c, d] = cross(part, part, wsem, 2 * c + d)
+            side(0)
+            for q in range(1, CHUNKS):
+                open_x(q)
+
+    def swap(c, i):
+        hc[c, i].wait_recv()
+        part = part_of(be, vs, c, slot[i])
+        fc[c, i] = cross(part, part, wsem, 2 * c + i)
 
     for f in fetch[5:]:
         f.wait()
@@ -199,16 +226,20 @@
             build(i * nt + b, LANES, [(tri, i + 1, b)], [(tri, i, b)])
 
     for j in near:
-        relay(j)
+        relay(0, j)
     build_edges(0)
     for j in near:
-        relay_side(j)
+        relay_side(0, j)
+    for q in range(1, CHUNKS):
+        open_rest(q)
+        side(q)
     build_edges(1)
     for b in range(0, nh, LANES):
         build(
             2 * nt + b, LANES, [(hin, 2, b), (hin, 3, b)], [(hin, 0, b), (hin, 1, b)]
         )
-    swap(0)
+    for i in range(2):
+        swap(0, i)
     keep.wait()
 
     for i in range(3):
@@ -229,32 +260,40 @@
     for c in range(3):
         bet[:, c * ext : c * ext + vs] = be[c, 0:vs].T
 
-    for j in range(hi):
-        ya[j].wait_recv()
-        yb[j].wait_recv()
-
     def decode(c, at, count, lanes):
-        dec[c, at : at + count, lanes] = mm(be[c, at : at + count], xs[:, lanes]).astype(BF)
+        here = pl.ds(at, count)
+        dec[c, here, lanes] = mm(be[c, here], xs[:, lanes]).astype(BF)
 
     def stretch(c, lanes):
         for r in range(0, 2 * nt + nh, 352):
             edge[c, r : r + 352, lanes] = mm(inct[r : r + 352], dec[c, :, lanes])
 
-    every = pl.ds(0, ff)
-    for c in range(3):
-        decode(c, 0, vs, every)
-        if c == 0:
-            swap(1)
+    def prepare(q):
+        lanes = pl.ds(q * pc, pc)
+        arrive(q)
+        for c in range(3):
+            decode(c, 0, vs, lanes)
+        for c in range(2):
+            if q == 0:
+                if c:
+                    for i in range(2):
+                        swap(c, i)
+                for i in range(2):
+                    fc[c, i].wait_recv()
+            decode(c, vs, 2 * halo, lanes)
+            stretch(c, lanes)
+
+    prepare(0)
     for c in range(2):
-        for d in range(2):
-            fc[c, d].wait_recv()
-        decode(c, vs, 2 * halo, every)
-        stretch(c, every)
         bet[:, c * ext + vs : (c + 1) * ext] = be[c, vs:ext].T
-    swap(2)
-    oc = cross(xs, xo, osem, 0)
-    for d in range(2):
-        fc[2, d].wait_recv()
+    for q in range(1, CHUNKS):
+        for j in near:
+            relay(q, j)
+            relay_side(q, j)
+    for i in range(2):
+        swap(2, i)
+    for i in range(2):
+        fc[2, i].wait_recv()
 
     k = 4.0 * MEMBRANE / frames
     kc, yc, pcs = {}, {}, {}
@@ -295,19 +334,27 @@
 
         lax.fori_loop(0, nh // step, bend_body, 0)
 
+    def back(q, c, i):
+        at = pl.multiple_of(c * ext + vs + slot[i] * halo, halo)
+        to = pl.multiple_of((1 - slot[i]) * halo, halo)
+        kc[q, c, i] = go(
+            adj.at[q, pl.ds(at, halo)], bk.at[q, c, pl.ds(to, halo)],
+            ksem, (q * 3 + c) * 2 + i, toward[i],
+        )
+
     for q in range(CHUNKS):
         lanes = pl.ds(q * pc, pc)
+        if q:
+            prepare(q)
         decode(2, vs, 2 * halo, lanes)
         stretch(2, lanes)
         elastic(q)
         for c in range(3):
             adj[q, c * ext + vs : (c + 1) * ext] = (mm(inc[vs:ext], force[c]) * k).astype(BF)
-            for d in range(2):
-                kc[q, c, d] = go(
-                    adj.at[q, pl.ds(c * ext + vs + d * halo, halo)],
-                    bk.at[q, c, pl.ds((1 - d) * halo, halo)],
-                    ksem, (q * 3 + c) * 2 + d, ring[d],
-                )
+            back(q, c, 1)
+            back(q, c, 0)
+        if q == CHUNKS - 1:
+            oc = cross(xs, xo, osem, 0)
         for c in range(3):
             part = mm(inc[0:vs], force[c]) * k
             if c == 2:
@@ -317,10 +364,10 @@
             adj[q, c * ext : c * ext + vs] = part.astype(BF)
         if q == 0:
             bet[:, 2 * ext + vs : 3 * ext] = be[2, vs:ext].T
-        for r in range(0, kk, tile):
-            g[q, r : r + tile] = mm(bet[r : r + tile], adj[q]).astype(BF)
         for j in order + [0]:
             hh = (h + j) % hi
+            here = pl.ds(pl.multiple_of(hh * PLANE * w, PLANE * w), PLANE * w)
+            g[q, here] = mm(bet[here], adj[q]).astype(BF)
             for i, ll in enumerate((loy, lod)):
                 at = pl.multiple_of((hh * PLANE + ll) * w, w)
                 yc[q, j, i] = go(
@@ -372,7 +419,8 @@
     def finish(q):
         s = gather_z(q, 0)
         rxc[q].wait_recv()
-        lg_ref[:, q * pc : (q + 1) * pc] = s + xl[q].astype(F32)
+        lg_ref[0, :, q * pc : (q + 1) * pc] = s
+        lg_ref[1, :, q * pc : (q + 1) * pc] = xl[q].astype(F32)
 
     def product(which, src, lat, c):
         for r in range(0, kk, tile):
@@ -417,7 +465,7 @@
         functools.partial(kernel, n, frames),
         out_shape=[
             jax.ShapeDtypeStruct((2, 3, vs // 2, kk), BF),
-            jax.ShapeDtypeStruct((w, ff), F32),
+            jax.ShapeDtypeStruct((2, w, ff), F32),
         ],
         in_specs=[hbm] * 9,
         out_specs=[vm] * 2,
@@ -457,9 +505,9 @@
             v((CHUNKS, w, pc), BF),
             v((CHUNKS, w, pc), BF),
             DMA((11,)),
-            DMA((2, 1)),
-            DMA((2, 2 * hi)),
-            DMA((2, 2 * hi)),
+            DMA((2, CHUNKS)),
+            DMA((2, CHUNKS * 2 * hi)),
+            DMA((2, CHUNKS * 2 * hi)),
             DMA((2, 2)),
             DMA((2, 6)),
             DMA((2, 6)),
@@ -474,10 +522,15 @@
             collective_id=0, has_side_effects=True, vmem_limit_bytes=52000 * 1024
         ),
     )(
-        latents.T, basis, rest_pos, triangles, hinges, rest_sq, bend_rest,
-        masses.reshape(1, vs), send_rows,
+        *(
+            pltpu.with_memory_space_constraint(a, pltpu.HBM)
+            for a in (
+                latents.T, basis, rest_pos, triangles, hinges, rest_sq, bend_rest,
+                masses.reshape(1, vs), send_rows,
+            )
+        )
     )
-    return (halves[0].astype(F32) + halves[1].astype(F32), lg.T)
+    return (halves[0].astype(F32) + halves[1].astype(F32), (lg[0] + lg[1]).T)
 
 
 def solution(mesh):

time: 77.3 us -> 69.2 us (0.90)
  local copies, waits for them, and re-layouts: 6.31 us -> 0 us
  Pallas kernels: 68.5 us -> 66.2 us
    unnamed x17 -> x0, local copies, waits for them, and re-layouts: 6.31 us -> none
    pallas_call x1, Pallas kernels: 68.5 us -> 66.2 us  [local(): pl.pallas_call(functools.partial(kernel, n, frames), out_shape=[jax.Shape...]
where the time goes in v3:
time: 69.2 us; the launch traced here: 69 us
  Pallas kernels  66.2 us (96%)
  other arithmetic  2.11 us (3%)
    pallas_call x1, Pallas kernels, local(): pl.pallas_call(functools.partial(kernel, n, frames), out_shape=[jax.Shape...  66.2 us
    add x1, other arithmetic, local(): return (halves[0].astype(F32) + halves[1].astype(F32), (lg[0] + lg[1]).T)  1.44 us

profile of v3, /device:TPU:0, one launch (start us, length us, event | category | flops | bytes accessed | tf_op | source)
XLA Modules:
  0.0 69.0 jit_solution(7532869983708034928)
XLA Ops:
  0.6 66.2 %shard_map.104 = (bf16[2,3,128,1024]{3,2,1,0:T(8,128)(2,1)S(1)}, f32[2,64,512]{2,1,0:T(8,128)S(1)}) custom-call(bf16[64,512]{1,0:T(8,128)(2,1)} %bitcast.8, bf16[3,256,1024]{2,1,0:T(8,128)(2,1)} %b_hbm.1, f32[3,256]{1,0:T(4,128)} %rest_hbm.1, s32[3,512]{1,0:T(4,128)} %tri_hbm.1, s32[4,384]{1,0:T(4,128)} %hin_hbm.1, f32[3,512]{1,0:T(4,128)} %rsq_hbm.1, ...), custom_call_target="tpu_custom_call" | custom-call | tf_op jit(solution)/shard_map/pallas_call | solution.py:464
  66.9 1.4 %add_bitcast_fusion = f32[3,128,1024]{2,1,0:T(8,128)} fusion(bf16[2,3,128,1024]{3,2,1,0:T(8,128)(2,1)S(1)} %get-tuple-element.4), kind=kLoop, calls=%fused_computation | loop fusion | flops 1179648 | bytes 3145728 | tf_op jit(solution)/shard_map/add | solution.py:533
  68.3 0.7 add_bitcast_fusion.1

commit v4 on v3

--- a/solution.py
+++ b/solution.py
@@ -283,13 +283,13 @@
             decode(c, vs, 2 * halo, lanes)
             stretch(c, lanes)
 
-    prepare(0)
-    for c in range(2):
-        bet[:, c * ext + vs : (c + 1) * ext] = be[c, vs:ext].T
     for q in range(1, CHUNKS):
         for j in near:
             relay(q, j)
             relay_side(q, j)
+    prepare(0)
+    for c in range(2):
+        bet[:, c * ext + vs : (c + 1) * ext] = be[c, vs:ext].T
     for i in range(2):
         swap(2, i)
     for i in range(2):
@@ -320,7 +320,7 @@
                     force[c, pl.ds(r2, step), pl.ds(t, LANES)] = (s2 * e2[c] + u).astype(BF)
             return carry
 
-        lax.fori_loop(0, nt // step, body, 0)
+        lax.fori_loop(0, nt // step, body, 0, unroll=4)
 
         def bend_body(i, carry):
             r = pl.multiple_of(2 * nt + i * step, step)
@@ -332,7 +332,7 @@
                     ).astype(BF)
             return carry
 
-        lax.fori_loop(0, nh // step, bend_body, 0)
+        lax.fori_loop(0, nh // step, bend_body, 0, unroll=4)
 
     def back(q, c, i):
         at = pl.multiple_of(c * ext + vs + slot[i] * halo, halo)

time: 69.2 us -> 69.1 us (level)
  no operation moved by 1% of the time
where the time goes in v4:
time: 69.1 us; the launch traced here: 68.9 us
  Pallas kernels  66.2 us (96%)
  other arithmetic  2.11 us (3%)
    pallas_call x1, Pallas kernels, local(): pl.pallas_call(functools.partial(kernel, n, frames), out_shape=[jax.Shape...  66.2 us
    add x1, other arithmetic, local(): return (halves[0].astype(F32) + halves[1].astype(F32), (lg[0] + lg[1]).T)  1.44 us

profile of v4, /device:TPU:0, one launch (start us, length us, event | category | flops | bytes accessed | tf_op | source)
XLA Modules:
  0.0 68.9 jit_solution(4909182611044017214)
XLA Ops:
  0.6 66.2 %shard_map.104 = (bf16[2,3,128,1024]{3,2,1,0:T(8,128)(2,1)S(1)}, f32[2,64,512]{2,1,0:T(8,128)S(1)}) custom-call(bf16[64,512]{1,0:T(8,128)(2,1)} %bitcast.8, bf16[3,256,1024]{2,1,0:T(8,128)(2,1)} %b_hbm.1, f32[3,256]{1,0:T(4,128)} %rest_hbm.1, s32[3,512]{1,0:T(4,128)} %tri_hbm.1, s32[4,384]{1,0:T(4,128)} %hin_hbm.1, f32[3,512]{1,0:T(4,128)} %rsq_hbm.1, ...), custom_call_target="tpu_custom_call" | custom-call | tf_op jit(solution)/shard_map/pallas_call | solution.py:464
  66.8 1.4 %add_bitcast_fusion = f32[3,128,1024]{2,1,0:T(8,128)} fusion(bf16[2,3,128,1024]{3,2,1,0:T(8,128)(2,1)S(1)} %get-tuple-element.4), kind=kLoop, calls=%fused_computation | loop fusion | flops 1179648 | bytes 3145728 | tf_op jit(solution)/shard_map/add | solution.py:533
  68.3 0.7 add_bitcast_fusion.1
